TPU v7x, 32 devices: a whole 2x2x4 slice. The times are simulated.
32 devices in a mesh: occ: 4 (over y, x), vir: 8 (over z, core).
Axes of the slice: x: 2, y: 2, z: 4, core: 2. Of those that a mesh axis runs over, the one named last changes fastest.
Arguments:
- amplitudes: bfloat16 [1504, 3072], P('occ', 'vir'), may hold values from -6 to 6
- integrals: bfloat16 [3072, 3072], P(None, 'vir'), may hold values from -0.15625 to 0.15625
- tile_block: int32 [24], replicated, may hold values from 0 to 5, as said below
- pair_mask: int32 [6, 6], replicated, may hold values 0 or 1
- partner: int32 [1504], P('occ'), may hold values from 0 to 1503, as said below
Outputs:
- residual: float32 [1504, 3072], P('occ', 'vir')
Inputs may be any that keep to these rules, and one draw needn't show every extreme that they name: partner is an involution without fixed points: partner[partner[r]] = r and partner[r] != r. tile_block never falls along the tiles, and each of the 6 blocks holds at least one tile.
All inputs are finite; a program needn't handle non-finite values.
Results may differ from a plain program's by a relative error of at most 0.0003.
Values may be sent and summed in bfloat16 or wider, within the bound.
No kernel may reach another device: no remote copies, remote signals or barrier semaphores. Data moves between devices by JAX's collectives and lax.ppermute only.
A program may use at most 128 MiB of HBM per device.

v0:
```python
import jax
import jax.numpy as jnp
from jax import lax
from jax.sharding import PartitionSpec as P

TILE = 128


def body(amplitudes, integrals, tile_block, pair_mask, partner):
    columns = integrals.shape[1]
    local_tiles = columns // TILE
    total_tiles = tile_block.shape[0]
    groups = pair_mask.shape[0]
    first_tile = lax.axis_index("vir") * local_tiles
    own_blocks = lax.dynamic_slice_in_dim(tile_block, first_tile, local_tiles)
    labels = jnp.arange(groups, dtype=jnp.int32)
    row_onehot = (tile_block[:, None] == labels[None, :]).astype(jnp.float32)
    col_onehot = (own_blocks[:, None] == labels[None, :]).astype(jnp.float32)
    live_tiles = jnp.dot(jnp.dot(row_onehot, pair_mask.astype(jnp.float32)), col_onehot.T)
    masked = (
        integrals.reshape(total_tiles, TILE, local_tiles, TILE)
        * live_tiles.astype(jnp.bfloat16)[:, None, :, None]
    )
    masked = masked.reshape(integrals.shape)
    own_count = amplitudes.shape[0]
    gathered = lax.all_gather(amplitudes, "occ", axis=0, tiled=True)
    partner_rows = jnp.take(gathered, partner, axis=0)
    stacked = jnp.concatenate((amplitudes, partner_rows), axis=0)
    pair_sums = jnp.dot(
        lax.all_gather(stacked, "vir", axis=1, tiled=True),
        masked,
        preferred_element_type=jnp.float32,
    )
    residual = pair_sums[:own_count] - pair_sums[own_count:]
    return residual


def solution(mesh):
    placed = (P("occ", "vir"), P(None, "vir"), P(), P(), P("occ"))
    return jax.shard_map(
        body, mesh=mesh, in_specs=placed, out_specs=P("occ", "vir"), check_vma=False
    )
```

profile of v0, /device:TPU:0, one launch (start us, length us, event | category | flops | bytes accessed | tf_op | source)
XLA Modules:
  0.0 107.5 jit_solution(9422348159117418414)
XLA Ops:
  6.5 0.0 all-gather.3.cloned.1.call-start
  6.5 0.7 all-gather.3.cloned.1.call-update
  7.3 0.0 all-gather.5.cloned.1.call-start
  7.3 0.7 compare_select_fusion
  8.0 0.7 compare_and_fusion
  8.7 30.6 %all-gather.3.cloned.1.call-done = bf16[1504,384]{1,0:T(8,128)(2,1)} async-done(((bf16[376,384]{1,0:T(8,128)(2,1)}), bf16[1504,384]{1,0:T(8,128)(2,1)}) %all-gather.3.cloned.1.call-update) | async-done | bytes 1155088 | tf_op jit(solution)/shard_map/all_gather | solution.py:26
  39.3 3.4 %gather_fusion = bf16[376,384]{1,0:T(8,128)(2,1)S(1)} fusion(bf16[1504,384]{1,0:T(8,128)(2,1)} %all-gather.3.cloned.1.call-done, s32[1024]{0:T(1024)S(1)} %pad_clamp_fusion), kind=kCustom, calls=%fused_computation | custom fusion | bytes 579040 | tf_op jit(solution)/shard_map/jit(_take)/gather | solution.py:27
  42.7 0.1 broadcast_select_fusion
  42.9 0.0 copy-done.2
  42.9 0.9 pad_maximum_fusion
  43.7 0.0 all-gather.5.cloned.1.call-update
  43.8 0.0 copy-done
  43.8 0.0 copy-start.4
  43.8 0.0 copy-start.3
  43.8 2.6 %copy.7 = bf16[3072,384]{0,1:T(8,128)(2,1)} copy(bf16[3072,384]{1,0:T(8,128)(2,1)S(1)} %copy-done) | data formatting | bytes 4718592 | tf_op args[1]
  46.4 0.0 copy-done.4
  46.4 0.1 dynamic_slice.3
  46.5 0.0 copy-done.3
  46.5 0.3 fusion.5
  46.8 47.7 %all-gather.5.cloned.1.call-done = bf16[752,3072]{1,0:T(8,128)(2,1)} async-done(((bf16[752,384]{1,0:T(8,128)(2,1)}), bf16[752,3072]{1,0:T(8,128)(2,1)}) %all-gather.5.cloned.1.call-update) | async-done | bytes 4620304 | tf_op jit(solution)/shard_map/all_gather | solution.py:30
  94.5 0.4 mul.15
  94.9 0.0 copy-done.1
  94.9 4.9 %fusion = f32[752,384]{1,0:T(8,128)S(1)} fusion(bf16[752,3072]{1,0:T(8,128)(2,1)} %all-gather.5.cloned.1.call-done, bf16[3072,384]{0,1:T(8,128)(2,1)S(1)} %copy-done.1, bf16[48,8,24,128]{3,2,1,0:T(8,128)(2,1)S(1)} %bitcast.8), kind=kOutput, calls=%fused_computation.2 | convolution fusion | flops 1775370240 | bytes 10493952 | tf_op jit(solution)/shard_map/dot_general | solution.py:29
  99.8 0.9 slice_subtract_fusion
  (4 shorter events, 0.0 us)
Async XLA Ops:
  6.5 36.3 %copy-start.2 = (bf16[376,384]{1,0:T(8,128)(2,1)S(1)}, bf16[376,384]{1,0:T(8,128)(2,1)}, u32[]{:S(2)}) copy-start(bf16[376,384]{1,0:T(8,128)(2,1)} %param.5) | copy-start | bytes 866308
  6.5 32.8 %all-gather.3.cloned.1.call-start = ((), (), s32[]{:S(2)}) async-start(), calls=%async_computation | async-start | bytes 1443840 | tf_op jit(solution)/shard_map/all_gather | solution.py:26
  7.3 87.3 %all-gather.5.cloned.1.call-start = ((), (), s32[]{:S(2)}) async-start(), calls=%async_computation.1 | async-start | bytes 5197824 | tf_op jit(solution)/shard_map/all_gather | solution.py:30
  8.7 35.1 %copy-start = (bf16[3072,384]{1,0:T(8,128)(2,1)S(1)}, bf16[3072,384]{1,0:T(8,128)(2,1)}, u32[]{:S(2)}) copy-start(bf16[3072,384]{1,0:T(8,128)(2,1)} %param.6) | copy-start | bytes 7077892
  43.8 2.7 %copy-start.4 = (s32[24]{0:T(128)S(1)}, s32[24]{0:T(128)}, u32[]{:S(2)}) copy-start(s32[24]{0:T(128)} %param.7) | copy-start | bytes 292
  43.8 2.7 %copy-start.3 = (s32[6,6]{1,0:T(8,128)S(1)}, s32[6,6]{1,0:T(8,128)}, u32[]{:S(2)}) copy-start(s32[6,6]{1,0:T(8,128)} %param.8) | copy-start | bytes 436
  46.4 48.5 %copy-start.1 = (bf16[3072,384]{0,1:T(8,128)(2,1)S(1)}, bf16[3072,384]{0,1:T(8,128)(2,1)}, u32[]{:S(2)}) copy-start(bf16[3072,384]{0,1:T(8,128)(2,1)} %copy.7) | copy-start | bytes 7077892
Sparse Core Ops, SparseCore 0:
  9.2 30.0 all-gather.2
  43.9 50.6 all-gather.4
where the time goes:
time: 108 us
  waiting for transfers between devices  79.1 us (73%)
  between operations  13.5 us (12%)
  local copies, waits for them, and re-layouts  6.49 us (6%)
  matrix products  5.19 us (5%)
  other arithmetic  3.24 us (3%)
    all_gather x1, waiting for transfers between devices, body(): lax.all_gather(stacked, 'vir', axis=1, tiled=True)  47.7 us
    all_gather x1, waiting for transfers between devices, body(): gathered = lax.all_gather(amplitudes, 'occ', axis=0, tiled=True)  30.6 us
    dot_general x1, matrix products, body(): jnp.dot(lax.all_gather(stacked, 'vir', axis=1, tiled=True), masked, prefe...  4.88 us
    gather x1, local copies, waits for them, and re-layouts, body(): partner_rows = jnp.take(gathered, partner, axis=0)  3.4 us
    unnamed x11, local copies, waits for them, and re-layouts  2.65 us
  transfers between devices with their start and end apart: 2, of which 2 were waited for; matrix products, arithmetic and copies ran while one was open for 4% of the time, Pallas kernels for 0%

commit v1 on v0

--- a/solution.py
+++ b/solution.py
@@ -4,6 +4,18 @@
 from jax.sharding import PartitionSpec as P
 
 TILE = 128
+
+
+def gather_around(array, axis, dim):
+    ways, here, step = (lax.axis_size(axis), lax.axis_index(axis), array.shape[dim])
+    shape = [n * ways if d == dim else n for d, n in enumerate(array.shape)]
+    full = lax.dynamic_update_slice_in_dim(
+        jnp.zeros(shape, array.dtype), array, here * step, axis=dim
+    )
+    for far in range(1, ways):
+        array = lax.ppermute(array, axis, [(d, (d + 1) % ways) for d in range(ways)])
+        full = lax.dynamic_update_slice_in_dim(full, array, (here - far) % ways * step, axis=dim)
+    return full
 
 
 def body(amplitudes, integrals, tile_block, pair_mask, partner):
@@ -27,9 +39,7 @@
     partner_rows = jnp.take(gathered, partner, axis=0)
     stacked = jnp.concatenate((amplitudes, partner_rows), axis=0)
     pair_sums = jnp.dot(
-        lax.all_gather(stacked, "vir", axis=1, tiled=True),
-        masked,
-        preferred_element_type=jnp.float32,
+        gather_around(stacked, "vir", 1), masked, preferred_element_type=jnp.float32
     )
     residual = pair_sums[:own_count] - pair_sums[own_count:]
     return residual

time: 108 us -> 140 us (1.30)
  waiting for transfers between devices: 79.1 us -> 95.9 us
  local copies, waits for them, and re-layouts: 6.49 us -> 21.6 us
    ppermute x0 -> x7, waiting for transfers between devices: none -> 64.5 us  [gather_around(): lax.ppermute(array, axis, [(d, (d + 1) % ways) for d in range(ways)])]
    all_gather x1 -> x0, waiting for transfers between devices: 47.7 us -> none  [body(): lax.all_gather(stacked, 'vir', axis=1, tiled=True)]
    dynamic_update_slice x0 -> x7, local copies, waits for them, and re-layouts: none -> 10.8 us  [gather_around(): lax.dynamic_update_slice_in_dim(full, array, (here - far) % ways * step,...]
    broadcast_in_dim x0 -> x1, local copies, waits for them, and re-layouts: none -> 2.68 us  [gather_around(): jnp.zeros(shape, array.dtype)]
    unnamed x11 -> x15, local copies, waits for them, and re-layouts: 2.65 us -> 4.33 us
  transfers between devices with their start and end apart: 2 -> 8, of which waited for: 2 -> 8; matrix products, arithmetic and copies ran while one was open for 4% -> 10% of each run, Pallas kernels for 0% -> 0%
where the time goes in v1:
time: 140 us
  waiting for transfers between devices  95.9 us (68%)
  local copies, waits for them, and re-layouts  21.6 us (15%)
  between operations  13.5 us (10%)
  matrix products  5.26 us (4%)
  other arithmetic  3.39 us (2%)
    ppermute x7, waiting for transfers between devices, gather_around(): lax.ppermute(array, axis, [(d, (d + 1) % ways) for d in range(ways)])  64.5 us
    all_gather x1, waiting for transfers between devices, body(): gathered = lax.all_gather(amplitudes, 'occ', axis=0, tiled=True)  30.7 us
    dynamic_update_slice x7, local copies, waits for them, and re-layouts, gather_around(): lax.dynamic_update_slice_in_dim(full, array, (here - far) % ways * step,...  10.8 us
    dot_general x1, matrix products, body(): jnp.dot(gather_around(stacked, 'vir', 1), masked, preferred_element_type=...  4.96 us
    unnamed x15, local copies, waits for them, and re-layouts  4.33 us
    gather x1, local copies, waits for them, and re-layouts, body(): partner_rows = jnp.take(gathered, partner, axis=0)  3.4 us
  transfers between devices with their start and end apart: 8, of which 8 were waited for; matrix products, arithmetic and copies ran while one was open for 10% of the time, Pallas kernels for 0%

profile of v1, /device:TPU:0, one launch (start us, length us, event | category | flops | bytes accessed | tf_op | source)
XLA Modules:
  0.0 139.7 jit_solution(12087572415335985815)
XLA Ops:
  6.5 0.7 all-gather.2.cloned.1.call-update
  8.6 30.7 %all-gather.2.cloned.1.call-done = bf16[1504,384]{1,0:T(8,128)(2,1)} async-done(((bf16[376,384]{1,0:T(8,128)(2,1)}), bf16[1504,384]{1,0:T(8,128)(2,1)}) %all-gather.2.cloned.1.call-update) | async-done | bytes 1155088 | tf_op jit(solution)/shard_map/all_gather | solution.py:38
  39.3 3.4 %gather_fusion = bf16[376,384]{1,0:T(8,128)(2,1)S(1)} fusion(bf16[1504,384]{1,0:T(8,128)(2,1)} %all-gather.2.cloned.1.call-done, s32[1024]{0:T(1024)S(1)} %pad_clamp_fusion), kind=kCustom, calls=%fused_computation | custom fusion | bytes 579040 | tf_op jit(solution)/shard_map/jit(_take)/gather | solution.py:39
  42.9 2.7 %broadcast_in_dim.20 = bf16[752,3072]{1,0:T(8,128)(2,1)} broadcast(bf16[]{:T(256)} %constant.68.clone.1), dimensions={} | broadcast | bytes 4620290 | tf_op jit(solution)/shard_map/broadcast_in_dim | solution.py:13
  45.6 1.0 pad_maximum_fusion
  46.6 11.0 %collective-permute-done = bf16[752,384]{1,0:T(8,128)(2,1)S(1)} collective-permute-done((bf16[752,384]{1,0:T(8,128)(2,1)S(1)}, bf16[752,384]{1,0:T(8,128)(2,1)S(1)}, u32[]{:S(2)}, u32[]{:S(2)}) %collective-permute-start) | collective-permute-done | bytes 577568 | tf_op jit(solution)/shard_map/ppermute | solution.py:16
  57.6 11.0 %collective-permute-done.1 = bf16[752,384]{1,0:T(8,128)(2,1)S(1)} collective-permute-done((bf16[752,384]{1,0:T(8,128)(2,1)S(1)}, bf16[752,384]{1,0:T(8,128)(2,1)S(1)}, u32[]{:S(2)}, u32[]{:S(2)}) %collective-permute-start.1) | collective-permute-done | bytes 577568 | tf_op jit(solution)/shard_map/ppermute | solution.py:16
  68.5 11.0 %collective-permute-done.2 = bf16[752,384]{1,0:T(8,128)(2,1)S(1)} collective-permute-done((bf16[752,384]{1,0:T(8,128)(2,1)S(1)}, bf16[752,384]{1,0:T(8,128)(2,1)S(1)}, u32[]{:S(2)}, u32[]{:S(2)}) %collective-permute-start.2) | collective-permute-done | bytes 577568 | tf_op jit(solution)/shard_map/ppermute | solution.py:16
  79.5 0.8 copy-done.3
  80.3 11.0 %collective-permute-done.3 = bf16[752,384]{1,0:T(8,128)(2,1)S(1)} collective-permute-done((bf16[752,384]{1,0:T(8,128)(2,1)S(1)}, bf16[752,384]{1,0:T(8,128)(2,1)S(1)}, u32[]{:S(2)}, u32[]{:S(2)}) %collective-permute-start.3) | collective-permute-done | bytes 577568 | tf_op jit(solution)/shard_map/ppermute | solution.py:16
  91.3 0.8 copy-done.4
  92.1 11.1 %collective-permute-done.4 = bf16[752,384]{1,0:T(8,128)(2,1)} collective-permute-done((bf16[752,384]{1,0:T(8,128)(2,1)S(1)}, bf16[752,384]{1,0:T(8,128)(2,1)}, u32[]{:S(2)}, u32[]{:S(2)}) %collective-permute-start.4) | collective-permute-done | bytes 577568 | tf_op jit(solution)/shard_map/ppermute | solution.py:16
  103.2 2.6 %copy.7 = bf16[3072,384]{0,1:T(8,128)(2,1)} copy(bf16[3072,384]{1,0:T(8,128)(2,1)S(1)} %copy-done) | data formatting | bytes 4718592 | tf_op args[1]
  106.3 0.9 constant_dynamic-update-slice_fusion.6
  107.2 7.3 %collective-permute-done.5 = bf16[752,384]{1,0:T(8,128)(2,1)} collective-permute-done((bf16[752,384]{1,0:T(8,128)(2,1)}, bf16[752,384]{1,0:T(8,128)(2,1)}, u32[]{:S(2)}, u32[]{:S(2)}) %collective-permute-start.5) | collective-permute-done | bytes 577568 | tf_op jit(solution)/shard_map/ppermute | solution.py:16
  114.5 0.9 constant_dynamic-update-slice_fusion.5
  115.5 2.0 %constant_dynamic-update-slice_fusion.4 = bf16[752,3072]{1,0:T(8,128)(2,1)} fusion(bf16[752,3072]{1,0:T(8,128)(2,1)} %constant_dynamic-update-slice_fusion.5, bf16[752,384]{1,0:T(8,128)(2,1)} %copy-done.3, s32[]{:T(128)S(6)} %select_n.75), kind=kLoop, calls=%fused_computation.20 | loop fusion | bytes 1155076 | tf_op jit(solution)/shard_map/dynamic_update_slice | solution.py:17
  117.5 2.0 %constant_dynamic-update-slice_fusion.3 = bf16[752,3072]{1,0:T(8,128)(2,1)} fusion(bf16[752,3072]{1,0:T(8,128)(2,1)} %constant_dynamic-update-slice_fusion.4, bf16[752,384]{1,0:T(8,128)(2,1)} %copy-done.4, s32[]{:T(128)S(6)} %select_n.77), kind=kLoop, calls=%fused_computation.19 | loop fusion | bytes 1155076 | tf_op jit(solution)/shard_map/dynamic_update_slice | solution.py:17
  119.4 2.0 %constant_dynamic-update-slice_fusion.2 = bf16[752,3072]{1,0:T(8,128)(2,1)} fusion(bf16[752,3072]{1,0:T(8,128)(2,1)} %constant_dynamic-update-slice_fusion.3, bf16[752,384]{1,0:T(8,128)(2,1)} %collective-permute-done.4, s32[]{:T(128)S(6)} %select_n.79), kind=kLoop, calls=%fused_computation.18 | loop fusion | bytes 1155076 | tf_op jit(solution)/shard_map/dynamic_update_slice | solution.py:17
  121.5 2.0 %constant_dynamic-update-slice_fusion.1 = bf16[752,3072]{1,0:T(8,128)(2,1)} fusion(bf16[752,3072]{1,0:T(8,128)(2,1)} %constant_dynamic-update-slice_fusion.2, bf16[752,384]{1,0:T(8,128)(2,1)} %collective-permute-done.5, s32[]{:T(128)S(6)} %select_n.81), kind=kLoop, calls=%fused_computation.17 | loop fusion | bytes 1155076 | tf_op jit(solution)/shard_map/dynamic_update_slice | solution.py:17
  123.5 2.2 %collective-permute-done.6 = bf16[752,384]{1,0:T(8,128)(2,1)S(1)} collective-permute-done((bf16[752,384]{1,0:T(8,128)(2,1)}, bf16[752,384]{1,0:T(8,128)(2,1)S(1)}, u32[]{:S(2)}, u32[]{:S(2)}) %collective-permute-start.6) | collective-permute-done | bytes 577568 | tf_op jit(solution)/shard_map/ppermute | solution.py:16
  125.7 0.9 constant_dynamic-update-slice_fusion
  127.0 5.0 %fusion = f32[752,384]{1,0:T(8,128)S(1)} fusion(bf16[752,3072]{1,0:T(8,128)(2,1)} %constant_dynamic-update-slice_fusion, bf16[3072,384]{0,1:T(8,128)(2,1)S(1)} %copy-done.1, bf16[48,8,24,128]{3,2,1,0:T(8,128)(2,1)S(1)} %bitcast.8), kind=kOutput, calls=%fused_computation.2 | convolution fusion | flops 1775370240 | bytes 10493952 | tf_op jit(solution)/shard_map/dot_general | solution.py:41
  131.9 0.9 slice_subtract_fusion
  (27 shorter events, 2.3 us)
Async XLA Ops:
  6.5 39.0 %copy-start.2 = (bf16[376,384]{1,0:T(8,128)(2,1)S(1)}, bf16[376,384]{1,0:T(8,128)(2,1)}, u32[]{:S(2)}) copy-start(bf16[376,384]{1,0:T(8,128)(2,1)} %param.5) | copy-start | bytes 866308
  6.5 32.8 %all-gather.2.cloned.1.call-start = ((), (), s32[]{:S(2)}) async-start(), calls=%async_computation | async-start | bytes 1443840 | tf_op jit(solution)/shard_map/all_gather | solution.py:38
  8.6 94.6 %copy-start = (bf16[3072,384]{1,0:T(8,128)(2,1)S(1)}, bf16[3072,384]{1,0:T(8,128)(2,1)}, u32[]{:S(2)}) copy-start(bf16[3072,384]{1,0:T(8,128)(2,1)} %param.6) | copy-start | bytes 7077892
  42.9 63.0 %copy-start.6 = (s32[24]{0:T(128)S(1)}, s32[24]{0:T(128)}, u32[]{:S(2)}) copy-start(s32[24]{0:T(128)} %param.7) | copy-start | bytes 292
  42.9 63.1 %copy-start.5 = (s32[6,6]{1,0:T(8,128)S(1)}, s32[6,6]{1,0:T(8,128)}, u32[]{:S(2)}) copy-start(s32[6,6]{1,0:T(8,128)} %param.8) | copy-start | bytes 436
  46.6 11.0 %collective-permute-start = (bf16[752,384]{1,0:T(8,128)(2,1)S(1)}, bf16[752,384]{1,0:T(8,128)(2,1)S(1)}, u32[]{:S(2)}, u32[]{:S(2)}) collective-permute-start(bf16[752,384]{1,0:T(8,128)(2,1)S(1)} %get-tuple-element.5), channel_id=1, source_target_pairs={{0,1},{1,2},{2,3},{3,4},{4,5},{5,6},{6,7},{7,0},{8,9},{9,10},{10,1... | collective-permute-start | bytes 1732616 | tf_op jit(solution)/shard_map/ppermute | solution.py:16
  57.6 11.0 %collective-permute-start.1 = (bf16[752,384]{1,0:T(8,128)(2,1)S(1)}, bf16[752,384]{1,0:T(8,128)(2,1)S(1)}, u32[]{:S(2)}, u32[]{:S(2)}) collective-permute-start(bf16[752,384]{1,0:T(8,128)(2,1)S(1)} %collective-permute-done), channel_id=1, source_target_pairs={{0,1},{1,2},{2,3},{3,4},{4,5},{5,6},{6,7},{7,0},{8,9},{9,10},{10,1... | collective-permute-start | bytes 1732616 | tf_op jit(solution)/shard_map/ppermute | solution.py:16
  68.5 11.0 %collective-permute-start.2 = (bf16[752,384]{1,0:T(8,128)(2,1)S(1)}, bf16[752,384]{1,0:T(8,128)(2,1)S(1)}, u32[]{:S(2)}, u32[]{:S(2)}) collective-permute-start(bf16[752,384]{1,0:T(8,128)(2,1)S(1)} %collective-permute-done.1), channel_id=1, source_target_pairs={{0,1},{1,2},{2,3},{3,4},{4,5},{5,6},{6,7},{7,0},{8,9},{9,10},{10,1... | collective-permute-start | bytes 1732616 | tf_op jit(solution)/shard_map/ppermute | solution.py:16
  79.5 0.8 copy-start.3
  80.3 11.0 %collective-permute-start.3 = (bf16[752,384]{1,0:T(8,128)(2,1)S(1)}, bf16[752,384]{1,0:T(8,128)(2,1)S(1)}, u32[]{:S(2)}, u32[]{:S(2)}) collective-permute-start(bf16[752,384]{1,0:T(8,128)(2,1)S(1)} %collective-permute-done.2), channel_id=1, source_target_pairs={{0,1},{1,2},{2,3},{3,4},{4,5},{5,6},{6,7},{7,0},{8,9},{9,10},{10,1... | collective-permute-start | bytes 1732616 | tf_op jit(solution)/shard_map/ppermute | solution.py:16
  91.3 0.9 copy-start.4
  92.1 11.1 %collective-permute-start.4 = (bf16[752,384]{1,0:T(8,128)(2,1)S(1)}, bf16[752,384]{1,0:T(8,128)(2,1)}, u32[]{:S(2)}, u32[]{:S(2)}) collective-permute-start(bf16[752,384]{1,0:T(8,128)(2,1)S(1)} %collective-permute-done.3), channel_id=1, source_target_pairs={{0,1},{1,2},{2,3},{3,4},{4,5},{5,6},{6,7},{7,0},{8,9},{9,10},{10,1... | collective-permute-start | bytes 1732616 | tf_op jit(solution)/shard_map/ppermute | solution.py:16
  103.2 11.3 %collective-permute-start.5 = (bf16[752,384]{1,0:T(8,128)(2,1)}, bf16[752,384]{1,0:T(8,128)(2,1)}, u32[]{:S(2)}, u32[]{:S(2)}) collective-permute-start(bf16[752,384]{1,0:T(8,128)(2,1)} %collective-permute-done.4), channel_id=1, source_target_pairs={{0,1},{1,2},{2,3},{3,4},{4,5},{5,6},{6,7},{7,0},{8,9},{9,10},{10,1... | collective-permute-start | bytes 1732616 | tf_op jit(solution)/shard_map/ppermute | solution.py:16
  107.2 19.8 %copy-start.1 = (bf16[3072,384]{0,1:T(8,128)(2,1)S(1)}, bf16[3072,384]{0,1:T(8,128)(2,1)}, u32[]{:S(2)}) copy-start(bf16[3072,384]{0,1:T(8,128)(2,1)} %copy.7) | copy-start | bytes 7077892
  114.5 11.2 %collective-permute-start.6 = (bf16[752,384]{1,0:T(8,128)(2,1)}, bf16[752,384]{1,0:T(8,128)(2,1)S(1)}, u32[]{:S(2)}, u32[]{:S(2)}) collective-permute-start(bf16[752,384]{1,0:T(8,128)(2,1)} %collective-permute-done.5), channel_id=1, source_target_pairs={{0,1},{1,2},{2,3},{3,4},{4,5},{5,6},{6,7},{7,0},{8,9},{9,10},{10,1... | collective-permute-start | bytes 1732616 | tf_op jit(solution)/shard_map/ppermute | solution.py:16
Sparse Core Ops, SparseCore 0:
  9.2 30.0 all-gather.1
